TPU v7x, 32 devices: a whole 2x2x4 slice. The times are simulated.
32 devices in a mesh: slab: 8 (over z, y), mem: 4 (over x, core).
Axes of the slice: x: 2, y: 2, z: 4, core: 2. Of those that a mesh axis runs over, the one named last changes fastest.
Arguments:
- starting_states_set: float32 [128, 64, 1024], P('mem', 'slab'), may hold values from -6 to 6
- land_mask: int32 [64, 1024], P('slab'), may hold values 0 or 1
- cell_class: int32 [64, 1024], P('slab'), may hold values from 0 to 7
- kappa_table: float32 [8], replicated, may hold values from 0.08 to 0.2
- flow_table: float32 [2, 8], replicated, may hold values from -0.3 to 0.3
- obs_index: int32 [1024], P('slab'), may hold values from 0 to 8191
- obs_values: float32 [1024], P('slab'), may hold values from -24 to 24
- obs_var: float32 [1024], P('slab'), may hold values from 0.1 to 1
Outputs:
- analysis: float32 [128, 64, 1024], P('mem', 'slab')
All inputs are finite; a program needn't handle non-finite values. No bound on the sum of `land_mask` on one device may be relied on, other than what follows from the above.
Results may differ from a plain program's by a relative error of at most 0.00016.
Values sent between devices are 32-bit elements; how exact they have to be, the bound alone decides.
A program may use at most 64 MiB of HBM per device.

v0:
```python
import jax
import jax.numpy as jnp
from jax import lax
from jax.sharding import PartitionSpec as P

STEPS = 8
ROOT_ITERATIONS = 8
NCLS = 8


def extended(block, sides, width):
    for axis, dim in sides:
        count = lax.axis_size(axis)
        forward = [(i, i + 1) for i in range(count - 1)]
        backward = [(target, source) for source, target in forward]
        low = lax.ppermute(
            lax.slice_in_dim(block, block.shape[dim] - width, None, axis=dim), axis, forward
        )
        high = lax.ppermute(lax.slice_in_dim(block, 0, width, axis=dim), axis, backward)
        block = jnp.concatenate([low, block, high], axis=dim)
    return block


def advance(center, north, south, diffusion, flow_east, flow_north, wet_cells):
    edge = jnp.zeros_like(center[..., :1])
    east = jnp.concatenate([center[..., 1:], edge], axis=-1)
    west = jnp.concatenate([edge, center[..., :-1]], axis=-1)
    spread = north + south + east + west - 4.0 * center
    return wet_cells * (
        center
        + diffusion * spread
        - 0.5 * flow_east * (east - west)
        - 0.5 * flow_north * (north - south)
    )


def coefficients(classes, mask_rows, kappa_table, flow_table):
    diffusion = jnp.zeros(classes.shape, jnp.float32)
    flow_east = jnp.zeros(classes.shape, jnp.float32)
    flow_north = jnp.zeros(classes.shape, jnp.float32)
    for label in range(NCLS):
        hit = classes == label
        diffusion = diffusion + jnp.where(hit, kappa_table[label], 0.0)
        flow_east = flow_east + jnp.where(hit, flow_table[0, label], 0.0)
        flow_north = flow_north + jnp.where(hit, flow_table[1, label], 0.0)
    return (diffusion, flow_east, flow_north, mask_rows.astype(jnp.float32))


def statistics(observed, values, variances, factor, ens_total):
    highest = lax.Precision.HIGHEST
    ybar = jnp.sum(observed, axis=0) / ens_total
    err = variances * factor
    anom = (observed - ybar) / jnp.sqrt(err * (ens_total - 1.0))
    dev = (values - ybar) / jnp.sqrt(err)
    return (jnp.dot(anom, anom.T, precision=highest), jnp.dot(anom, dev, precision=highest))


def local(
    starting_states_set,
    land_mask,
    cell_class,
    kappa_table,
    flow_table,
    obs_index,
    obs_values,
    obs_var,
):
    highest = lax.Precision.HIGHEST
    kd = starting_states_set.shape[0]
    rows = starting_states_set.shape[1]
    ens_total = kd * lax.axis_size("mem")
    current_profile = starting_states_set
    diffusion, flow_east, flow_north, wet_cells = coefficients(
        cell_class, land_mask, kappa_table, flow_table
    )
    for step in range(STEPS):
        padded = extended(current_profile, (("slab", 1),), 1)
        current_profile = advance(
            padded[:, 1:-1],
            padded[:, 2:],
            padded[:, :-2],
            diffusion,
            flow_east,
            flow_north,
            wet_cells,
        )
    raveled_vector = current_profile.reshape(kd, rows * current_profile.shape[2])
    observed = jnp.take(raveled_vector, obs_index, axis=1)
    slab_here = lax.axis_index("slab").astype(jnp.float32)
    factor = 1.0 + 2.0 * slab_here / float(lax.axis_size("slab") - 1)
    member_group = lax.axis_index("mem")
    columns = lax.all_to_all(observed, "mem", split_axis=1, concat_axis=0, tiled=True)
    count = columns.shape[1]
    values = lax.dynamic_slice_in_dim(obs_values, member_group * count, count)
    variances = lax.dynamic_slice_in_dim(obs_var, member_group * count, count)
    gram_part, proj_part = statistics(columns, values, variances, factor, ens_total)
    gram, proj = lax.psum((gram_part, proj_part), ("slab", "mem"))
    ident = jnp.eye(ens_total, dtype=jnp.float32)
    matrix = ident + gram
    scale = jnp.trace(matrix)
    upper = matrix / scale
    lower = ident
    for turn in range(ROOT_ITERATIONS):
        factor_q = 1.5 * ident - 0.5 * jnp.dot(lower, upper, precision=highest)
        upper = jnp.dot(upper, factor_q, precision=highest)
        lower = jnp.dot(factor_q, lower, precision=highest)
    transform_weights = lower / jnp.sqrt(scale)
    mean_w = jnp.dot(lower, jnp.dot(lower, proj, precision=highest), precision=highest) / (
        scale * jnp.sqrt(ens_total - 1.0)
    )
    total_w = transform_weights + mean_w[:, None]
    omega = 1.0 / ens_total + total_w - (jnp.sum(total_w, axis=0) / ens_total)[None, :]
    mixed = jnp.einsum(
        "ij,irc->jrc",
        omega,
        lax.all_to_all(current_profile, "mem", split_axis=2, concat_axis=0, tiled=True),
        precision=highest,
    )
    return lax.all_to_all(mixed, "mem", split_axis=0, concat_axis=2, tiled=True)


def solution(mesh):
    return jax.shard_map(
        local,
        mesh=mesh,
        in_specs=(
            P("mem", "slab", None),
            P("slab", None),
            P("slab", None),
            P(),
            P(),
            P("slab"),
            P("slab"),
            P("slab"),
        ),
        out_specs=P("mem", "slab", None),
        check_vma=False,
    )
```

profile of v0, /device:TPU:0, one launch (start us, length us, event | category | flops | bytes accessed | tf_op | source)
XLA Modules:
  0.0 308.6 jit_solution(16976725727790895447)
XLA Ops:
  6.5 1.9 copy.42
  8.4 0.7 fusion.44
  9.2 1.3 collective-permute-start
  10.5 5.5 %collective-permute-start.1 = (f32[32,1,1024]{2,0,1:T(8,128)}, f32[32,1,1024]{2,0,1:T(8,128)S(1)}, u32[]{:S(2)}, u32[]{:S(2)}) collective-permute-start(f32[32,1,1024]{2,0,1:T(8,128)} %get-tuple-element.42), channel_id=1, source_target_pairs={{0,4},{4,8},{8,12},{12,16},{16,20},{20,24},{24,28},{1,5},{5,9},{9,... | collective-permute-start | bytes 393224 | tf_op jit(solution)/shard_map/ppermute | solution.py:16
  16.4 0.7 fusion.47
  17.0 0.7 fusion.46
  17.8 5.0 %select_add_fusion = (f32[8,1024]{1,0:T(8,128)S(1)}, pred[8,1024]{1,0:T(8,128)(4,1)S(1)}, pred[8,1024]{1,0:T(8,128)(4,1)S(1)}, pred[8,1024]{1,0:T(8,128)(4,1)S(1...) fusion(f32[]{:T(128)} %bitcast.7, f32[]{:T(128)} %bitcast.6, ...), kind=kLoop, calls=%fused_computation.61 | loop fusion | flops 188416 | bytes 131104 | tf_op jit(solution)/shard_map/add | solution.py:43
  22.8 5.0 %add_multiply_fusion = f32[8,1024]{1,0:T(8,128)S(1)} fusion(pred[8,1024]{1,0:T(8,128)(4,1)S(1)} %get-tuple-element.13, pred[8,1024]{1,0:T(8,128)(4,1)S(1)} %get-tuple-element.12, pred[8,1024]{1,0:T(8,128)(4,1)S(1)} %get-tuple-element.11, pred[8,1024]{1,0:T(8,128)(4,1)S(1)} %get-tuple-element.10, pred[8,1024]{1,0:T(8,128)(4,1)S(1)} %get-tuple-element.9, ...), kind=kLoop, calls=%fused_computation.59 | loop fusion | flops 131072 | bytes 98336 | tf_op jit(solution)/shard_map/mul | solution.py:33
  27.8 5.0 %add_multiply_fusion.1 = f32[8,1024]{1,0:T(8,128)S(1)} fusion(pred[8,1024]{1,0:T(8,128)(4,1)S(1)} %get-tuple-element.13, pred[8,1024]{1,0:T(8,128)(4,1)S(1)} %get-tuple-element.12, pred[8,1024]{1,0:T(8,128)(4,1)S(1)} %get-tuple-element.11, pred[8,1024]{1,0:T(8,128)(4,1)S(1)} %get-tuple-element.10, pred[8,1024]{1,0:T(8,128)(4,1)S(1)} %get-tuple-element.9, ...), kind=kLoop, calls=%fused_computation.60 | loop fusion | flops 131072 | bytes 98336 | tf_op jit(solution)/shard_map/mul | solution.py:32
  33.0 0.6 subtract_multiply_fusion.7
  33.7 1.3 collective-permute-start.2
  35.0 5.4 %collective-permute-start.3 = (f32[32,1,1024]{2,0,1:T(8,128)S(1)}, f32[32,1,1024]{2,0,1:T(8,128)S(1)}, u32[]{:S(2)}, u32[]{:S(2)}) collective-permute-start(f32[32,1,1024]{2,0,1:T(8,128)S(1)} %get-tuple-element.38), channel_id=1, source_target_pairs={{0,4},{4,8},{8,12},{12,16},{16,20},{20,24},{24,28},{1,5},{5,9},{9,... | collective-permute-start | bytes 393224 | tf_op jit(solution)/shard_map/ppermute | solution.py:16
  41.4 2.9 collective-permute-done.3
  44.4 0.7 subtract_multiply_fusion.6
  45.1 1.3 collective-permute-start.4
  46.4 5.0 %collective-permute-start.5 = (f32[32,1,1024]{2,0,1:T(8,128)S(1)}, f32[32,1,1024]{2,0,1:T(8,128)S(1)}, u32[]{:S(2)}, u32[]{:S(2)}) collective-permute-start(f32[32,1,1024]{2,0,1:T(8,128)S(1)} %get-tuple-element.34), channel_id=1, source_target_pairs={{0,4},{4,8},{8,12},{12,16},{16,20},{20,24},{24,28},{1,5},{5,9},{9,... | collective-permute-start | bytes 393224 | tf_op jit(solution)/shard_map/ppermute | solution.py:16
  51.8 1.1 collective-permute-done.4
  52.9 3.0 collective-permute-done.5
  55.8 0.7 subtract_multiply_fusion.5
  56.5 1.3 collective-permute-start.6
  57.8 5.0 %collective-permute-start.7 = (f32[32,1,1024]{2,0,1:T(8,128)S(1)}, f32[32,1,1024]{2,0,1:T(8,128)S(1)}, u32[]{:S(2)}, u32[]{:S(2)}) collective-permute-start(f32[32,1,1024]{2,0,1:T(8,128)S(1)} %get-tuple-element.30), channel_id=1, source_target_pairs={{0,4},{4,8},{8,12},{12,16},{16,20},{20,24},{24,28},{1,5},{5,9},{9,... | collective-permute-start | bytes 393224 | tf_op jit(solution)/shard_map/ppermute | solution.py:16
  63.3 1.3 collective-permute-done.6
  64.6 3.0 collective-permute-done.7
  67.5 0.7 subtract_multiply_fusion.4
  68.2 1.3 collective-permute-start.8
  69.5 5.0 %collective-permute-start.9 = (f32[32,1,1024]{2,0,1:T(8,128)S(1)}, f32[32,1,1024]{2,0,1:T(8,128)S(1)}, u32[]{:S(2)}, u32[]{:S(2)}) collective-permute-start(f32[32,1,1024]{2,0,1:T(8,128)S(1)} %get-tuple-element.26), channel_id=1, source_target_pairs={{0,4},{4,8},{8,12},{12,16},{16,20},{20,24},{24,28},{1,5},{5,9},{9,... | collective-permute-start | bytes 393224 | tf_op jit(solution)/shard_map/ppermute | solution.py:16
  75.0 1.3 collective-permute-done.8
  76.3 3.0 collective-permute-done.9
  79.3 0.7 subtract_multiply_fusion.3
  80.0 1.3 collective-permute-start.10
  81.3 5.0 %collective-permute-start.11 = (f32[32,1,1024]{2,0,1:T(8,128)S(1)}, f32[32,1,1024]{2,0,1:T(8,128)S(1)}, u32[]{:S(2)}, u32[]{:S(2)}) collective-permute-start(f32[32,1,1024]{2,0,1:T(8,128)S(1)} %get-tuple-element.22), channel_id=1, source_target_pairs={{0,4},{4,8},{8,12},{12,16},{16,20},{20,24},{24,28},{1,5},{5,9},{9,... | collective-permute-start | bytes 393224 | tf_op jit(solution)/shard_map/ppermute | solution.py:16
  86.7 1.3 collective-permute-done.10
  88.0 3.0 collective-permute-done.11
  91.0 0.7 subtract_multiply_fusion.2
  91.7 1.3 collective-permute-start.12
  93.0 5.0 %collective-permute-start.13 = (f32[32,1,1024]{2,0,1:T(8,128)S(1)}, f32[32,1,1024]{2,0,1:T(8,128)S(1)}, u32[]{:S(2)}, u32[]{:S(2)}) collective-permute-start(f32[32,1,1024]{2,0,1:T(8,128)S(1)} %get-tuple-element.18), channel_id=1, source_target_pairs={{0,4},{4,8},{8,12},{12,16},{16,20},{20,24},{24,28},{1,5},{5,9},{9,... | collective-permute-start | bytes 393224 | tf_op jit(solution)/shard_map/ppermute | solution.py:16
  98.4 1.3 collective-permute-done.12
  99.7 3.0 collective-permute-done.13
  102.7 0.7 subtract_multiply_fusion.1
  103.4 1.3 collective-permute-start.14
  104.7 5.0 %collective-permute-start.15 = (f32[32,1,1024]{2,0,1:T(8,128)S(1)}, f32[32,1,1024]{2,0,1:T(8,128)S(1)}, u32[]{:S(2)}, u32[]{:S(2)}) collective-permute-start(f32[32,1,1024]{2,0,1:T(8,128)S(1)} %get-tuple-element.14), channel_id=1, source_target_pairs={{0,4},{4,8},{8,12},{12,16},{16,20},{20,24},{24,28},{1,5},{5,9},{9,... | collective-permute-start | bytes 393224 | tf_op jit(solution)/shard_map/ppermute | solution.py:16
  110.1 1.3 collective-permute-done.14
  111.5 3.0 collective-permute-done.15
  114.4 0.7 subtract_multiply_fusion
  115.1 2.6 copy.43
  117.7 2.8 gather_fusion
  120.7 0.7 reshape.69
  121.4 3.4 %all-to-all-start = ((f32[4,1,1024]{2,1,0:T(1,128)}), f32[4,1,1024]{2,1,0:T(1,128)S(1)}, u32[]{:S(2)}, u32[]{:S(2)}) async-start(f32[4,1,1024]{2,1,0:T(1,128)} %reshape.69), calls=%async_computation | async-start | bytes 32768 | tf_op jit(solution)/shard_map/all_to_all | solution.py:92
  124.9 2.7 copy.46
  127.6 4.8 %reshape.67 = f32[4,1,65536]{2,1,0:T(1,128)} reshape(f32[1024,8,32]{2,1,0:T(8,128)} %bitcast.117) | data formatting | bytes 2097152
  132.4 3.5 %all-to-all-start.1 = ((f32[4,1,65536]{2,1,0:T(1,128)}), f32[4,1,65536]{2,1,0:T(1,128)S(1)}, u32[]{:S(2)}, u32[]{:S(2)}) async-start(f32[4,1,65536]{2,1,0:T(1,128)} %reshape.67), calls=%async_computation.1 | async-start | bytes 2097152 | tf_op jit(solution)/shard_map/all_to_all | solution.py:116
  136.6 0.7 reduce.3
  137.9 0.9 fusion.49
  139.1 44.7 %psum.15 = f32[128]{0:T(128)S(1)} all-reduce(f32[128]{0:T(128)S(1)} %convolution_bitcast_fusion.2), channel_id=1, replica_groups=mesh['slab'=8,'mem'=4] {'slab','mem'}, use_global_device_ids=true, to_apply=%region_3.4 | all-reduce | flops 128 | bytes 1024 | tf_op jit(solution)/shard_map/psum | solution.py:97
  183.8 76.2 %all-reduce.18.cloned.1.call-done = f32[128,128]{1,0:T(8,128)} async-done(((f32[128,128]{1,0:T(8,128)}), f32[128,128]{1,0:T(8,128)}) %all-reduce.18.cloned.1.call-update) | async-done | bytes 65552 | tf_op jit(solution)/shard_map/psum | solution.py:97
  259.9 1.5 select_reduce_fusion
  261.4 1.6 fusion.7
  263.2 1.6 fusion.17
  270.8 3.7 %reduce.2 = f32[4,65536]{1,0:T(4,128)S(1)} reduce(f32[4,1,65536]{2,1,0:T(1,128)S(1)} %all-to-all-done.1, f32[]{:T(128)} %broadcast.130), dimensions={1}, to_apply=%all_to_all.41.reduce_sub_computation | reduce | bytes 2097156 | tf_op jit(solution)/shard_map/all_to_all | solution.py:116
  274.5 3.4 %reshape.68 = f32[1024,8,32]{2,1,0:T(8,128)} reshape(f32[4,65536]{1,0:T(4,128)S(1)} %reduce.2) | data formatting | bytes 2097152
  277.9 2.8 copy.47
  280.7 1.1 fusion.9
  282.4 18.2 %all_to_all.52 = f32[128,8,256]{2,1,0:T(8,128)S(1)} all-to-all(f32[128,8,256]{2,1,0:T(8,128)S(1)} %copy.49), channel_id=1, replica_groups=mesh['slab'=8,'mem'=4] {'mem'}, dimensions={0} | all-to-all | bytes 2097152 | tf_op jit(solution)/shard_map/all_to_all | solution.py:119
  300.6 1.1 copy.50
  (80 shorter events, 11.0 us)
Async XLA Ops:
  6.5 9.8 %copy-start.2 = (f32[8]{0:T(128)S(1)}, f32[8]{0:T(128)}, u32[]{:S(2)}) copy-start(f32[8]{0:T(128)} %param.11) | copy-start | bytes 100
  6.5 10.5 %copy-start = (f32[2,8]{1,0:T(2,128)S(1)}, f32[2,8]{1,0:T(2,128)}, u32[]{:S(2)}) copy-start(f32[2,8]{1,0:T(2,128)} %param.12) | copy-start | bytes 196
  6.5 11.2 %copy-start.5 = (s32[128]{0:T(128)S(1)}, s32[128]{0:T(128)}, u32[]{:S(2)}) copy-start(s32[128]{0:T(128)} %param.13) | copy-start | bytes 1540
  6.5 11.2 %copy-start.3 = (s32[8,1024]{1,0:T(8,128)S(1)}, s32[8,1024]{1,0:T(8,128)}, u32[]{:S(2)}) copy-start(s32[8,1024]{1,0:T(8,128)} %param.10) | copy-start | bytes 98308
  6.5 26.3 %copy-start.1 = (s32[8,1024]{1,0:T(8,128)S(1)}, s32[8,1024]{1,0:T(8,128)}, u32[]{:S(2)}) copy-start(s32[8,1024]{1,0:T(8,128)} %param.9) | copy-start | bytes 98308
  9.2 23.8 %collective-permute-start = (f32[32,1,1024]{2,0,1:T(8,128)}, f32[32,1,1024]{2,0,1:T(8,128)S(1)}, u32[]{:S(2)}, u32[]{:S(2)}) collective-permute-start(f32[32,1,1024]{2,0,1:T(8,128)} %get-tuple-element.43), channel_id=1, source_target_pairs={{4,0},{8,4},{12,8},{16,12},{20,16},{24,20},{28,24},{5,1},{9,5},{13... | collective-permute-start | bytes 393224 | tf_op jit(solution)/shard_map/ppermute | solution.py:19
  10.5 22.5 %collective-permute-start.1 = (f32[32,1,1024]{2,0,1:T(8,128)}, f32[32,1,1024]{2,0,1:T(8,128)S(1)}, u32[]{:S(2)}, u32[]{:S(2)}) collective-permute-start(f32[32,1,1024]{2,0,1:T(8,128)} %get-tuple-element.42), channel_id=1, source_target_pairs={{0,4},{4,8},{8,12},{12,16},{16,20},{20,24},{24,28},{1,5},{5,9},{9,... | collective-permute-start | bytes 393224 | tf_op jit(solution)/shard_map/ppermute | solution.py:16
  33.7 7.8 %collective-permute-start.2 = (f32[32,1,1024]{2,0,1:T(8,128)S(1)}, f32[32,1,1024]{2,0,1:T(8,128)S(1)}, u32[]{:S(2)}, u32[]{:S(2)}) collective-permute-start(f32[32,1,1024]{2,0,1:T(8,128)S(1)} %get-tuple-element.39), channel_id=1, source_target_pairs={{4,0},{8,4},{12,8},{16,12},{20,16},{24,20},{28,24},{5,1},{9,5},{13... | collective-permute-start | bytes 393224 | tf_op jit(solution)/shard_map/ppermute | solution.py:19
  35.0 9.4 %collective-permute-start.3 = (f32[32,1,1024]{2,0,1:T(8,128)S(1)}, f32[32,1,1024]{2,0,1:T(8,128)S(1)}, u32[]{:S(2)}, u32[]{:S(2)}) collective-permute-start(f32[32,1,1024]{2,0,1:T(8,128)S(1)} %get-tuple-element.38), channel_id=1, source_target_pairs={{0,4},{4,8},{8,12},{12,16},{16,20},{20,24},{24,28},{1,5},{5,9},{9,... | collective-permute-start | bytes 393224 | tf_op jit(solution)/shard_map/ppermute | solution.py:16
  45.1 7.8 %collective-permute-start.4 = (f32[32,1,1024]{2,0,1:T(8,128)S(1)}, f32[32,1,1024]{2,0,1:T(8,128)S(1)}, u32[]{:S(2)}, u32[]{:S(2)}) collective-permute-start(f32[32,1,1024]{2,0,1:T(8,128)S(1)} %get-tuple-element.35), channel_id=1, source_target_pairs={{4,0},{8,4},{12,8},{16,12},{20,16},{24,20},{28,24},{5,1},{9,5},{13... | collective-permute-start | bytes 393224 | tf_op jit(solution)/shard_map/ppermute | solution.py:19
  46.4 9.5 %collective-permute-start.5 = (f32[32,1,1024]{2,0,1:T(8,128)S(1)}, f32[32,1,1024]{2,0,1:T(8,128)S(1)}, u32[]{:S(2)}, u32[]{:S(2)}) collective-permute-start(f32[32,1,1024]{2,0,1:T(8,128)S(1)} %get-tuple-element.34), channel_id=1, source_target_pairs={{0,4},{4,8},{8,12},{12,16},{16,20},{20,24},{24,28},{1,5},{5,9},{9,... | collective-permute-start | bytes 393224 | tf_op jit(solution)/shard_map/ppermute | solution.py:16
  56.5 8.1 %collective-permute-start.6 = (f32[32,1,1024]{2,0,1:T(8,128)S(1)}, f32[32,1,1024]{2,0,1:T(8,128)S(1)}, u32[]{:S(2)}, u32[]{:S(2)}) collective-permute-start(f32[32,1,1024]{2,0,1:T(8,128)S(1)} %get-tuple-element.31), channel_id=1, source_target_pairs={{4,0},{8,4},{12,8},{16,12},{20,16},{24,20},{28,24},{5,1},{9,5},{13... | collective-permute-start | bytes 393224 | tf_op jit(solution)/shard_map/ppermute | solution.py:19
  57.8 9.7 %collective-permute-start.7 = (f32[32,1,1024]{2,0,1:T(8,128)S(1)}, f32[32,1,1024]{2,0,1:T(8,128)S(1)}, u32[]{:S(2)}, u32[]{:S(2)}) collective-permute-start(f32[32,1,1024]{2,0,1:T(8,128)S(1)} %get-tuple-element.30), channel_id=1, source_target_pairs={{0,4},{4,8},{8,12},{12,16},{16,20},{20,24},{24,28},{1,5},{5,9},{9,... | collective-permute-start | bytes 393224 | tf_op jit(solution)/shard_map/ppermute | solution.py:16
  68.2 8.1 %collective-permute-start.8 = (f32[32,1,1024]{2,0,1:T(8,128)S(1)}, f32[32,1,1024]{2,0,1:T(8,128)S(1)}, u32[]{:S(2)}, u32[]{:S(2)}) collective-permute-start(f32[32,1,1024]{2,0,1:T(8,128)S(1)} %get-tuple-element.27), channel_id=1, source_target_pairs={{4,0},{8,4},{12,8},{16,12},{20,16},{24,20},{28,24},{5,1},{9,5},{13... | collective-permute-start | bytes 393224 | tf_op jit(solution)/shard_map/ppermute | solution.py:19
  69.5 9.7 %collective-permute-start.9 = (f32[32,1,1024]{2,0,1:T(8,128)S(1)}, f32[32,1,1024]{2,0,1:T(8,128)S(1)}, u32[]{:S(2)}, u32[]{:S(2)}) collective-permute-start(f32[32,1,1024]{2,0,1:T(8,128)S(1)} %get-tuple-element.26), channel_id=1, source_target_pairs={{0,4},{4,8},{8,12},{12,16},{16,20},{20,24},{24,28},{1,5},{5,9},{9,... | collective-permute-start | bytes 393224 | tf_op jit(solution)/shard_map/ppermute | solution.py:16
  80.0 8.1 %collective-permute-start.10 = (f32[32,1,1024]{2,0,1:T(8,128)S(1)}, f32[32,1,1024]{2,0,1:T(8,128)S(1)}, u32[]{:S(2)}, u32[]{:S(2)}) collective-permute-start(f32[32,1,1024]{2,0,1:T(8,128)S(1)} %get-tuple-element.23), channel_id=1, source_target_pairs={{4,0},{8,4},{12,8},{16,12},{20,16},{24,20},{28,24},{5,1},{9,5},{13... | collective-permute-start | bytes 393224 | tf_op jit(solution)/shard_map/ppermute | solution.py:19
  81.3 9.7 %collective-permute-start.11 = (f32[32,1,1024]{2,0,1:T(8,128)S(1)}, f32[32,1,1024]{2,0,1:T(8,128)S(1)}, u32[]{:S(2)}, u32[]{:S(2)}) collective-permute-start(f32[32,1,1024]{2,0,1:T(8,128)S(1)} %get-tuple-element.22), channel_id=1, source_target_pairs={{0,4},{4,8},{8,12},{12,16},{16,20},{20,24},{24,28},{1,5},{5,9},{9,... | collective-permute-start | bytes 393224 | tf_op jit(solution)/shard_map/ppermute | solution.py:16
  91.7 8.1 %collective-permute-start.12 = (f32[32,1,1024]{2,0,1:T(8,128)S(1)}, f32[32,1,1024]{2,0,1:T(8,128)S(1)}, u32[]{:S(2)}, u32[]{:S(2)}) collective-permute-start(f32[32,1,1024]{2,0,1:T(8,128)S(1)} %get-tuple-element.19), channel_id=1, source_target_pairs={{4,0},{8,4},{12,8},{16,12},{20,16},{24,20},{28,24},{5,1},{9,5},{13... | collective-permute-start | bytes 393224 | tf_op jit(solution)/shard_map/ppermute | solution.py:19
  93.0 9.7 %collective-permute-start.13 = (f32[32,1,1024]{2,0,1:T(8,128)S(1)}, f32[32,1,1024]{2,0,1:T(8,128)S(1)}, u32[]{:S(2)}, u32[]{:S(2)}) collective-permute-start(f32[32,1,1024]{2,0,1:T(8,128)S(1)} %get-tuple-element.18), channel_id=1, source_target_pairs={{0,4},{4,8},{8,12},{12,16},{16,20},{20,24},{24,28},{1,5},{5,9},{9,... | collective-permute-start | bytes 393224 | tf_op jit(solution)/shard_map/ppermute | solution.py:16
  103.4 8.1 %collective-permute-start.14 = (f32[32,1,1024]{2,0,1:T(8,128)S(1)}, f32[32,1,1024]{2,0,1:T(8,128)S(1)}, u32[]{:S(2)}, u32[]{:S(2)}) collective-permute-start(f32[32,1,1024]{2,0,1:T(8,128)S(1)} %get-tuple-element.15), channel_id=1, source_target_pairs={{4,0},{8,4},{12,8},{16,12},{20,16},{24,20},{28,24},{5,1},{9,5},{13... | collective-permute-start | bytes 393224 | tf_op jit(solution)/shard_map/ppermute | solution.py:19
  104.7 9.7 %collective-permute-start.15 = (f32[32,1,1024]{2,0,1:T(8,128)S(1)}, f32[32,1,1024]{2,0,1:T(8,128)S(1)}, u32[]{:S(2)}, u32[]{:S(2)}) collective-permute-start(f32[32,1,1024]{2,0,1:T(8,128)S(1)} %get-tuple-element.14), channel_id=1, source_target_pairs={{0,4},{4,8},{8,12},{12,16},{16,20},{20,24},{24,28},{1,5},{5,9},{9,... | collective-permute-start | bytes 393224 | tf_op jit(solution)/shard_map/ppermute | solution.py:16
  114.4 10.4 %copy-start.4 = (f32[128]{0:T(128)S(1)}, f32[128]{0:T(128)}, u32[]{:S(2)}) copy-start(f32[128]{0:T(128)} %param.15) | copy-start | bytes 1540
  121.4 11.1 %all-to-all-start = ((f32[4,1,1024]{2,1,0:T(1,128)}), f32[4,1,1024]{2,1,0:T(1,128)S(1)}, u32[]{:S(2)}, u32[]{:S(2)}) async-start(f32[4,1,1024]{2,1,0:T(1,128)} %reshape.69), calls=%async_computation | async-start | bytes 32768 | tf_op jit(solution)/shard_map/all_to_all | solution.py:92
  127.6 11.3 %copy-start.6 = (f32[128]{0:T(128)S(1)}, f32[128]{0:T(128)}, u32[]{:S(2)}) copy-start(f32[128]{0:T(128)} %param.14) | copy-start | bytes 1540
  132.4 138.3 %all-to-all-start.1 = ((f32[4,1,65536]{2,1,0:T(1,128)}), f32[4,1,65536]{2,1,0:T(1,128)S(1)}, u32[]{:S(2)}, u32[]{:S(2)}) async-start(f32[4,1,65536]{2,1,0:T(1,128)} %reshape.67), calls=%async_computation.1 | async-start | bytes 2097152 | tf_op jit(solution)/shard_map/all_to_all | solution.py:116
  136.0 124.0 %all-reduce.18.cloned.1.call-start = ((), (), s32[]{:S(2)}) async-start(), calls=%async_computation.3 | async-start | bytes 131072 | tf_op jit(solution)/shard_map/psum | solution.py:97
Sparse Core Ops, SparseCore 0:
  142.4 117.4 all-reduce.17
where the time goes:
time: 310 us; the launch traced here: 309 us
  waiting for transfers between devices  105 us (34%)
  blocking collectives  62.9 us (20%)
  starting transfers between devices  58.4 us (19%)
  local copies, waits for them, and re-layouts  29.9 us (10%)
  other arithmetic  26.7 us (9%)
  between operations  15.3 us (5%)
  matrix products  10.1 us (3%)
    psum x1, waiting for transfers between devices, local(): gram, proj = lax.psum((gram_part, proj_part), ('slab', 'mem'))  76.2 us
    psum x1, blocking collectives, local(): gram, proj = lax.psum((gram_part, proj_part), ('slab', 'mem'))  44.7 us
    ppermute x8, starting transfers between devices, extended(): lax.ppermute(lax.slice_in_dim(block, block.shape[dim] - width, None, axis...  41.1 us
    ppermute x8, waiting for transfers between devices, extended(): lax.ppermute(lax.slice_in_dim(block, block.shape[dim] - width, None, axis...  20.7 us
    all_to_all x1, blocking collectives, local(): return lax.all_to_all(mixed, 'mem', split_axis=0, concat_axis=2, tiled=True)  18.2 us
    unnamed x19, local copies, waits for them, and re-layouts  10.9 us
    ppermute x8, starting transfers between devices, extended(): lax.ppermute(lax.slice_in_dim(block, 0, width, axis=dim), axis, backward)  10.3 us
    ppermute x8, waiting for transfers between devices, extended(): lax.ppermute(lax.slice_in_dim(block, 0, width, axis=dim), axis, backward)  8.4 us
  transfers between devices with their start and end apart: 19, of which 15 were waited for; matrix products, arithmetic and copies ran while one was open for 13% of the time, Pallas kernels for 0%

commit v1 on v0

--- a/solution.py
+++ b/solution.py
@@ -6,6 +6,16 @@
 STEPS = 8
 ROOT_ITERATIONS = 8
 NCLS = 8
+
+
+def turn_the_samples(my_data, mesh_dim="mem"):
+    mid_arr = jnp.concatenate(
+        lax.all_to_all(
+            jnp.stack(jnp.split(my_data, lax.axis_size(mesh_dim), axis=2), axis=0), mesh_dim, 0, 0
+        ),
+        axis=0,
+    )
+    return mid_arr
 
 
 def extended(block, sides, width):
@@ -110,12 +120,7 @@
     )
     total_w = transform_weights + mean_w[:, None]
     omega = 1.0 / ens_total + total_w - (jnp.sum(total_w, axis=0) / ens_total)[None, :]
-    mixed = jnp.einsum(
-        "ij,irc->jrc",
-        omega,
-        lax.all_to_all(current_profile, "mem", split_axis=2, concat_axis=0, tiled=True),
-        precision=highest,
-    )
+    mixed = jnp.einsum("ij,irc->jrc", omega, turn_the_samples(current_profile), precision=highest)
     return lax.all_to_all(mixed, "mem", split_axis=0, concat_axis=2, tiled=True)
 
 

time: 310 us -> 299 us (0.965)
  local copies, waits for them, and re-layouts: 29.9 us -> 17 us
    unnamed x19 -> x17, local copies, waits for them, and re-layouts: 10.9 us -> 2.71 us
    all_to_all x1 -> x0, other arithmetic: 3.71 us -> none  [local(): lax.all_to_all(current_profile, 'mem', split_axis=2, concat_axis=0, tiled...]
    all_to_all x2 -> x1, local copies, waits for them, and re-layouts: 3.38 us -> 0.08 us  [turn_the_samples(): lax.all_to_all(jnp.stack(jnp.split(my_data, lax.axis_size(mesh_dim), axis...]
  transfers between devices with their start and end apart: 19 -> 19, of which waited for: 15 -> 16; matrix products, arithmetic and copies ran while one was open for 13% -> 12% of each run, Pallas kernels for 0% -> 0%
where the time goes in v1:
time: 299 us; the launch traced here: 297 us
  waiting for transfers between devices  108 us (36%)
  blocking collectives  62.9 us (21%)
  starting transfers between devices  58.4 us (20%)
  other arithmetic  25.3 us (8%)
  local copies, waits for them, and re-layouts  17 us (6%)
  between operations  15.5 us (5%)
  matrix products  10.3 us (3%)
    psum x1, waiting for transfers between devices, local(): gram, proj = lax.psum((gram_part, proj_part), ('slab', 'mem'))  76.2 us
    psum x1, blocking collectives, local(): gram, proj = lax.psum((gram_part, proj_part), ('slab', 'mem'))  44.7 us
    ppermute x8, starting transfers between devices, extended(): lax.ppermute(lax.slice_in_dim(block, block.shape[dim] - width, None, axis...  41.1 us
    ppermute x8, waiting for transfers between devices, extended(): lax.ppermute(lax.slice_in_dim(block, block.shape[dim] - width, None, axis...  20.7 us
    all_to_all x1, blocking collectives, local(): return lax.all_to_all(mixed, 'mem', split_axis=0, concat_axis=2, tiled=True)  18.2 us
    ppermute x8, starting transfers between devices, extended(): lax.ppermute(lax.slice_in_dim(block, 0, width, axis=dim), axis, backward)  10.3 us
    ppermute x8, waiting for transfers between devices, extended(): lax.ppermute(lax.slice_in_dim(block, 0, width, axis=dim), axis, backward)  8.4 us
  transfers between devices with their start and end apart: 19, of which 16 were waited for; matrix products, arithmetic and copies ran while one was open for 12% of the time, Pallas kernels for 0%

profile of v1, /device:TPU:0, one launch (start us, length us, event | category | flops | bytes accessed | tf_op | source)
XLA Modules:
  0.0 297.3 jit_solution(5623991947786902906)
XLA Ops:
  6.6 1.9 copy.26
  8.5 0.7 fusion.44
  9.2 1.3 collective-permute-start
  10.5 5.5 %collective-permute-start.1 = (f32[32,1,1024]{2,0,1:T(8,128)}, f32[32,1,1024]{2,0,1:T(8,128)S(1)}, u32[]{:S(2)}, u32[]{:S(2)}) collective-permute-start(f32[32,1,1024]{2,0,1:T(8,128)} %get-tuple-element.46), channel_id=1, source_target_pairs={{0,4},{4,8},{8,12},{12,16},{16,20},{20,24},{24,28},{1,5},{5,9},{9,... | collective-permute-start | bytes 393224 | tf_op jit(solution)/shard_map/ppermute | solution.py:26
  17.0 0.7 fusion.47
  17.6 0.7 fusion.46
  18.3 4.9 %select_add_fusion = (f32[8,1024]{1,0:T(8,128)S(1)}, pred[8,1024]{1,0:T(8,128)(4,1)S(1)}, pred[8,1024]{1,0:T(8,128)(4,1)S(1)}, pred[8,1024]{1,0:T(8,128)(4,1)S(1...) fusion(f32[]{:T(128)} %bitcast.7, f32[]{:T(128)} %bitcast.6, ...), kind=kLoop, calls=%fused_computation.66 | loop fusion | flops 188416 | bytes 131104 | tf_op jit(solution)/shard_map/add | solution.py:53
  23.3 5.0 %add_multiply_fusion = f32[8,1024]{1,0:T(8,128)S(1)} fusion(pred[8,1024]{1,0:T(8,128)(4,1)S(1)} %get-tuple-element.13, pred[8,1024]{1,0:T(8,128)(4,1)S(1)} %get-tuple-element.12, pred[8,1024]{1,0:T(8,128)(4,1)S(1)} %get-tuple-element.11, pred[8,1024]{1,0:T(8,128)(4,1)S(1)} %get-tuple-element.10, pred[8,1024]{1,0:T(8,128)(4,1)S(1)} %get-tuple-element.9, ...), kind=kLoop, calls=%fused_computation.64 | loop fusion | flops 131072 | bytes 98336 | tf_op jit(solution)/shard_map/mul | solution.py:43
  28.3 5.1 %add_multiply_fusion.1 = f32[8,1024]{1,0:T(8,128)S(1)} fusion(pred[8,1024]{1,0:T(8,128)(4,1)S(1)} %get-tuple-element.13, pred[8,1024]{1,0:T(8,128)(4,1)S(1)} %get-tuple-element.12, pred[8,1024]{1,0:T(8,128)(4,1)S(1)} %get-tuple-element.11, pred[8,1024]{1,0:T(8,128)(4,1)S(1)} %get-tuple-element.10, pred[8,1024]{1,0:T(8,128)(4,1)S(1)} %get-tuple-element.9, ...), kind=kLoop, calls=%fused_computation.65 | loop fusion | flops 131072 | bytes 98336 | tf_op jit(solution)/shard_map/mul | solution.py:42
  33.4 0.8 convert_element_type.10
  34.2 0.7 broadcast_in_dim.152
  35.0 0.6 subtract_multiply_fusion.7
  35.6 1.3 collective-permute-start.2
  36.9 5.4 %collective-permute-start.3 = (f32[32,1,1024]{2,0,1:T(8,128)S(1)}, f32[32,1,1024]{2,0,1:T(8,128)S(1)}, u32[]{:S(2)}, u32[]{:S(2)}) collective-permute-start(f32[32,1,1024]{2,0,1:T(8,128)S(1)} %get-tuple-element.42), channel_id=1, source_target_pairs={{0,4},{4,8},{8,12},{12,16},{16,20},{20,24},{24,28},{1,5},{5,9},{9,... | collective-permute-start | bytes 393224 | tf_op jit(solution)/shard_map/ppermute | solution.py:26
  43.4 2.9 collective-permute-done.3
  46.3 0.7 subtract_multiply_fusion.6
  47.0 1.3 collective-permute-start.4
  48.3 5.0 %collective-permute-start.5 = (f32[32,1,1024]{2,0,1:T(8,128)S(1)}, f32[32,1,1024]{2,0,1:T(8,128)S(1)}, u32[]{:S(2)}, u32[]{:S(2)}) collective-permute-start(f32[32,1,1024]{2,0,1:T(8,128)S(1)} %get-tuple-element.38), channel_id=1, source_target_pairs={{0,4},{4,8},{8,12},{12,16},{16,20},{20,24},{24,28},{1,5},{5,9},{9,... | collective-permute-start | bytes 393224 | tf_op jit(solution)/shard_map/ppermute | solution.py:26
  53.7 1.1 collective-permute-done.4
  54.8 3.0 collective-permute-done.5
  57.8 0.7 subtract_multiply_fusion.5
  58.5 1.3 collective-permute-start.6
  59.8 5.0 %collective-permute-start.7 = (f32[32,1,1024]{2,0,1:T(8,128)S(1)}, f32[32,1,1024]{2,0,1:T(8,128)S(1)}, u32[]{:S(2)}, u32[]{:S(2)}) collective-permute-start(f32[32,1,1024]{2,0,1:T(8,128)S(1)} %get-tuple-element.34), channel_id=1, source_target_pairs={{0,4},{4,8},{8,12},{12,16},{16,20},{20,24},{24,28},{1,5},{5,9},{9,... | collective-permute-start | bytes 393224 | tf_op jit(solution)/shard_map/ppermute | solution.py:26
  65.2 1.3 collective-permute-done.6
  66.5 3.0 collective-permute-done.7
  69.5 0.7 subtract_multiply_fusion.4
  70.2 1.3 collective-permute-start.8
  71.5 5.0 %collective-permute-start.9 = (f32[32,1,1024]{2,0,1:T(8,128)S(1)}, f32[32,1,1024]{2,0,1:T(8,128)S(1)}, u32[]{:S(2)}, u32[]{:S(2)}) collective-permute-start(f32[32,1,1024]{2,0,1:T(8,128)S(1)} %get-tuple-element.30), channel_id=1, source_target_pairs={{0,4},{4,8},{8,12},{12,16},{16,20},{20,24},{24,28},{1,5},{5,9},{9,... | collective-permute-start | bytes 393224 | tf_op jit(solution)/shard_map/ppermute | solution.py:26
  76.9 1.3 collective-permute-done.8
  78.3 3.0 collective-permute-done.9
  81.2 0.7 subtract_multiply_fusion.3
  81.9 1.3 collective-permute-start.10
  83.2 5.0 %collective-permute-start.11 = (f32[32,1,1024]{2,0,1:T(8,128)S(1)}, f32[32,1,1024]{2,0,1:T(8,128)S(1)}, u32[]{:S(2)}, u32[]{:S(2)}) collective-permute-start(f32[32,1,1024]{2,0,1:T(8,128)S(1)} %get-tuple-element.26), channel_id=1, source_target_pairs={{0,4},{4,8},{8,12},{12,16},{16,20},{20,24},{24,28},{1,5},{5,9},{9,... | collective-permute-start | bytes 393224 | tf_op jit(solution)/shard_map/ppermute | solution.py:26
  88.6 1.3 collective-permute-done.10
  90.0 3.0 collective-permute-done.11
  92.9 0.7 subtract_multiply_fusion.2
  93.6 1.3 collective-permute-start.12
  94.9 5.0 %collective-permute-start.13 = (f32[32,1,1024]{2,0,1:T(8,128)S(1)}, f32[32,1,1024]{2,0,1:T(8,128)S(1)}, u32[]{:S(2)}, u32[]{:S(2)}) collective-permute-start(f32[32,1,1024]{2,0,1:T(8,128)S(1)} %get-tuple-element.22), channel_id=1, source_target_pairs={{0,4},{4,8},{8,12},{12,16},{16,20},{20,24},{24,28},{1,5},{5,9},{9,... | collective-permute-start | bytes 393224 | tf_op jit(solution)/shard_map/ppermute | solution.py:26
  100.4 1.3 collective-permute-done.12
  101.7 3.0 collective-permute-done.13
  104.7 0.7 subtract_multiply_fusion.1
  105.4 1.3 collective-permute-start.14
  106.7 5.0 %collective-permute-start.15 = (f32[32,1,1024]{2,0,1:T(8,128)S(1)}, f32[32,1,1024]{2,0,1:T(8,128)S(1)}, u32[]{:S(2)}, u32[]{:S(2)}) collective-permute-start(f32[32,1,1024]{2,0,1:T(8,128)S(1)} %get-tuple-element.18), channel_id=1, source_target_pairs={{0,4},{4,8},{8,12},{12,16},{16,20},{20,24},{24,28},{1,5},{5,9},{9,... | collective-permute-start | bytes 393224 | tf_op jit(solution)/shard_map/ppermute | solution.py:26
  112.1 1.3 collective-permute-done.14
  113.4 3.0 collective-permute-done.15
  116.4 0.7 subtract_multiply_fusion
  117.0 2.7 copy.27
  119.8 2.8 gather_fusion
  122.8 0.7 reshape.71
  123.5 3.2 %all-to-all-start = ((f32[4,1,1024]{2,1,0:T(1,128)}), f32[4,1,1024]{2,1,0:T(1,128)S(1)}, u32[]{:S(2)}, u32[]{:S(2)}) async-start(f32[4,1,1024]{2,1,0:T(1,128)} %reshape.71), calls=%async_computation | async-start | bytes 32768 | tf_op jit(solution)/shard_map/all_to_all | solution.py:102
  126.7 1.0 pad_maximum_fusion.16
  127.8 2.8 all-to-all-done
  130.5 3.5 %all-to-all-start.1 = ((f32[4,32,8,256]{3,1,2,0:T(8,128)}), f32[4,32,8,256]{3,1,2,0:T(8,128)S(1)}, u32[]{:S(2)}, u32[]{:S(2)}) async-start(f32[4,32,8,256]{3,1,2,0:T(8,128)} %pad_maximum_fusion.16), calls=%async_computation.1 | async-start | bytes 2097152 | tf_op jit(solution)/shard_map/all_to_all | solution.py:13
  134.8 0.6 reduce.2
  136.0 0.9 fusion.49
  137.2 44.7 %psum.15 = f32[128]{0:T(128)S(1)} all-reduce(f32[128]{0:T(128)S(1)} %convolution_bitcast_fusion.2), channel_id=1, replica_groups=mesh['slab'=8,'mem'=4] {'slab','mem'}, use_global_device_ids=true, to_apply=%region_3.4 | all-reduce | flops 128 | bytes 1024 | tf_op jit(solution)/shard_map/psum | solution.py:107
  181.9 76.2 %all-reduce.18.cloned.1.call-done = f32[128,128]{1,0:T(8,128)} async-done(((f32[128,128]{1,0:T(8,128)}), f32[128,128]{1,0:T(8,128)}) %all-reduce.18.cloned.1.call-update) | async-done | bytes 65552 | tf_op jit(solution)/shard_map/psum | solution.py:107
  258.0 1.5 select_reduce_fusion
  259.6 1.7 fusion.7
  261.4 1.7 fusion.17
  269.5 1.1 fusion.9
  270.6 0.6 copy.32
  271.2 18.2 %all_to_all.39 = f32[128,8,256]{2,1,0:T(8,128)S(1)} all-to-all(f32[128,8,256]{2,1,0:T(8,128)S(1)} %copy.32), channel_id=1, replica_groups=mesh['slab'=8,'mem'=4] {'mem'}, dimensions={0} | all-to-all | bytes 2097152 | tf_op jit(solution)/shard_map/all_to_all | solution.py:124
  289.4 1.1 copy.33
  (78 shorter events, 11.1 us)
Async XLA Ops:
  6.5 9.8 %copy-start.5 = (s32[128]{0:T(128)S(1)}, s32[128]{0:T(128)}, u32[]{:S(2)}) copy-start(s32[128]{0:T(128)} %param.13) | copy-start | bytes 1540
  6.5 10.4 %copy-start.1 = (f32[8]{0:T(128)S(1)}, f32[8]{0:T(128)}, u32[]{:S(2)}) copy-start(f32[8]{0:T(128)} %param.11) | copy-start | bytes 100
  6.5 11.1 %copy-start = (f32[2,8]{1,0:T(2,128)S(1)}, f32[2,8]{1,0:T(2,128)}, u32[]{:S(2)}) copy-start(f32[2,8]{1,0:T(2,128)} %param.12) | copy-start | bytes 196
  6.5 11.8 %copy-start.2 = (s32[8,1024]{1,0:T(8,128)S(1)}, s32[8,1024]{1,0:T(8,128)}, u32[]{:S(2)}) copy-start(s32[8,1024]{1,0:T(8,128)} %param.10) | copy-start | bytes 98308
  6.5 26.8 %copy-start.3 = (f32[128]{0:T(128)S(1)}, f32[128]{0:T(128)}, u32[]{:S(2)}) copy-start(f32[128]{0:T(128)} %param.15) | copy-start | bytes 1540
  9.2 25.8 %collective-permute-start = (f32[32,1,1024]{2,0,1:T(8,128)}, f32[32,1,1024]{2,0,1:T(8,128)S(1)}, u32[]{:S(2)}, u32[]{:S(2)}) collective-permute-start(f32[32,1,1024]{2,0,1:T(8,128)} %get-tuple-element.47), channel_id=1, source_target_pairs={{4,0},{8,4},{12,8},{16,12},{20,16},{24,20},{28,24},{5,1},{9,5},{13... | collective-permute-start | bytes 393224 | tf_op jit(solution)/shard_map/ppermute | solution.py:29
  10.5 24.5 %collective-permute-start.1 = (f32[32,1,1024]{2,0,1:T(8,128)}, f32[32,1,1024]{2,0,1:T(8,128)S(1)}, u32[]{:S(2)}, u32[]{:S(2)}) collective-permute-start(f32[32,1,1024]{2,0,1:T(8,128)} %get-tuple-element.46), channel_id=1, source_target_pairs={{0,4},{4,8},{8,12},{12,16},{16,20},{20,24},{24,28},{1,5},{5,9},{9,... | collective-permute-start | bytes 393224 | tf_op jit(solution)/shard_map/ppermute | solution.py:26
  35.6 7.8 %collective-permute-start.2 = (f32[32,1,1024]{2,0,1:T(8,128)S(1)}, f32[32,1,1024]{2,0,1:T(8,128)S(1)}, u32[]{:S(2)}, u32[]{:S(2)}) collective-permute-start(f32[32,1,1024]{2,0,1:T(8,128)S(1)} %get-tuple-element.43), channel_id=1, source_target_pairs={{4,0},{8,4},{12,8},{16,12},{20,16},{24,20},{28,24},{5,1},{9,5},{13... | collective-permute-start | bytes 393224 | tf_op jit(solution)/shard_map/ppermute | solution.py:29
  36.9 9.4 %collective-permute-start.3 = (f32[32,1,1024]{2,0,1:T(8,128)S(1)}, f32[32,1,1024]{2,0,1:T(8,128)S(1)}, u32[]{:S(2)}, u32[]{:S(2)}) collective-permute-start(f32[32,1,1024]{2,0,1:T(8,128)S(1)} %get-tuple-element.42), channel_id=1, source_target_pairs={{0,4},{4,8},{8,12},{12,16},{16,20},{20,24},{24,28},{1,5},{5,9},{9,... | collective-permute-start | bytes 393224 | tf_op jit(solution)/shard_map/ppermute | solution.py:26
  47.0 7.8 %collective-permute-start.4 = (f32[32,1,1024]{2,0,1:T(8,128)S(1)}, f32[32,1,1024]{2,0,1:T(8,128)S(1)}, u32[]{:S(2)}, u32[]{:S(2)}) collective-permute-start(f32[32,1,1024]{2,0,1:T(8,128)S(1)} %get-tuple-element.39), channel_id=1, source_target_pairs={{4,0},{8,4},{12,8},{16,12},{20,16},{24,20},{28,24},{5,1},{9,5},{13... | collective-permute-start | bytes 393224 | tf_op jit(solution)/shard_map/ppermute | solution.py:29
  48.3 9.5 %collective-permute-start.5 = (f32[32,1,1024]{2,0,1:T(8,128)S(1)}, f32[32,1,1024]{2,0,1:T(8,128)S(1)}, u32[]{:S(2)}, u32[]{:S(2)}) collective-permute-start(f32[32,1,1024]{2,0,1:T(8,128)S(1)} %get-tuple-element.38), channel_id=1, source_target_pairs={{0,4},{4,8},{8,12},{12,16},{16,20},{20,24},{24,28},{1,5},{5,9},{9,... | collective-permute-start | bytes 393224 | tf_op jit(solution)/shard_map/ppermute | solution.py:26
  58.5 8.1 %collective-permute-start.6 = (f32[32,1,1024]{2,0,1:T(8,128)S(1)}, f32[32,1,1024]{2,0,1:T(8,128)S(1)}, u32[]{:S(2)}, u32[]{:S(2)}) collective-permute-start(f32[32,1,1024]{2,0,1:T(8,128)S(1)} %get-tuple-element.35), channel_id=1, source_target_pairs={{4,0},{8,4},{12,8},{16,12},{20,16},{24,20},{28,24},{5,1},{9,5},{13... | collective-permute-start | bytes 393224 | tf_op jit(solution)/shard_map/ppermute | solution.py:29
  59.8 9.7 %collective-permute-start.7 = (f32[32,1,1024]{2,0,1:T(8,128)S(1)}, f32[32,1,1024]{2,0,1:T(8,128)S(1)}, u32[]{:S(2)}, u32[]{:S(2)}) collective-permute-start(f32[32,1,1024]{2,0,1:T(8,128)S(1)} %get-tuple-element.34), channel_id=1, source_target_pairs={{0,4},{4,8},{8,12},{12,16},{16,20},{20,24},{24,28},{1,5},{5,9},{9,... | collective-permute-start | bytes 393224 | tf_op jit(solution)/shard_map/ppermute | solution.py:26
  70.2 8.1 %collective-permute-start.8 = (f32[32,1,1024]{2,0,1:T(8,128)S(1)}, f32[32,1,1024]{2,0,1:T(8,128)S(1)}, u32[]{:S(2)}, u32[]{:S(2)}) collective-permute-start(f32[32,1,1024]{2,0,1:T(8,128)S(1)} %get-tuple-element.31), channel_id=1, source_target_pairs={{4,0},{8,4},{12,8},{16,12},{20,16},{24,20},{28,24},{5,1},{9,5},{13... | collective-permute-start | bytes 393224 | tf_op jit(solution)/shard_map/ppermute | solution.py:29
  71.5 9.7 %collective-permute-start.9 = (f32[32,1,1024]{2,0,1:T(8,128)S(1)}, f32[32,1,1024]{2,0,1:T(8,128)S(1)}, u32[]{:S(2)}, u32[]{:S(2)}) collective-permute-start(f32[32,1,1024]{2,0,1:T(8,128)S(1)} %get-tuple-element.30), channel_id=1, source_target_pairs={{0,4},{4,8},{8,12},{12,16},{16,20},{20,24},{24,28},{1,5},{5,9},{9,... | collective-permute-start | bytes 393224 | tf_op jit(solution)/shard_map/ppermute | solution.py:26
  81.9 8.1 %collective-permute-start.10 = (f32[32,1,1024]{2,0,1:T(8,128)S(1)}, f32[32,1,1024]{2,0,1:T(8,128)S(1)}, u32[]{:S(2)}, u32[]{:S(2)}) collective-permute-start(f32[32,1,1024]{2,0,1:T(8,128)S(1)} %get-tuple-element.27), channel_id=1, source_target_pairs={{4,0},{8,4},{12,8},{16,12},{20,16},{24,20},{28,24},{5,1},{9,5},{13... | collective-permute-start | bytes 393224 | tf_op jit(solution)/shard_map/ppermute | solution.py:29
  83.2 9.7 %collective-permute-start.11 = (f32[32,1,1024]{2,0,1:T(8,128)S(1)}, f32[32,1,1024]{2,0,1:T(8,128)S(1)}, u32[]{:S(2)}, u32[]{:S(2)}) collective-permute-start(f32[32,1,1024]{2,0,1:T(8,128)S(1)} %get-tuple-element.26), channel_id=1, source_target_pairs={{0,4},{4,8},{8,12},{12,16},{16,20},{20,24},{24,28},{1,5},{5,9},{9,... | collective-permute-start | bytes 393224 | tf_op jit(solution)/shard_map/ppermute | solution.py:26
  93.6 8.1 %collective-permute-start.12 = (f32[32,1,1024]{2,0,1:T(8,128)S(1)}, f32[32,1,1024]{2,0,1:T(8,128)S(1)}, u32[]{:S(2)}, u32[]{:S(2)}) collective-permute-start(f32[32,1,1024]{2,0,1:T(8,128)S(1)} %get-tuple-element.23), channel_id=1, source_target_pairs={{4,0},{8,4},{12,8},{16,12},{20,16},{24,20},{28,24},{5,1},{9,5},{13... | collective-permute-start | bytes 393224 | tf_op jit(solution)/shard_map/ppermute | solution.py:29
  94.9 9.7 %collective-permute-start.13 = (f32[32,1,1024]{2,0,1:T(8,128)S(1)}, f32[32,1,1024]{2,0,1:T(8,128)S(1)}, u32[]{:S(2)}, u32[]{:S(2)}) collective-permute-start(f32[32,1,1024]{2,0,1:T(8,128)S(1)} %get-tuple-element.22), channel_id=1, source_target_pairs={{0,4},{4,8},{8,12},{12,16},{16,20},{20,24},{24,28},{1,5},{5,9},{9,... | collective-permute-start | bytes 393224 | tf_op jit(solution)/shard_map/ppermute | solution.py:26
  105.4 8.1 %collective-permute-start.14 = (f32[32,1,1024]{2,0,1:T(8,128)S(1)}, f32[32,1,1024]{2,0,1:T(8,128)S(1)}, u32[]{:S(2)}, u32[]{:S(2)}) collective-permute-start(f32[32,1,1024]{2,0,1:T(8,128)S(1)} %get-tuple-element.19), channel_id=1, source_target_pairs={{4,0},{8,4},{12,8},{16,12},{20,16},{24,20},{28,24},{5,1},{9,5},{13... | collective-permute-start | bytes 393224 | tf_op jit(solution)/shard_map/ppermute | solution.py:29
  106.7 9.7 %collective-permute-start.15 = (f32[32,1,1024]{2,0,1:T(8,128)S(1)}, f32[32,1,1024]{2,0,1:T(8,128)S(1)}, u32[]{:S(2)}, u32[]{:S(2)}) collective-permute-start(f32[32,1,1024]{2,0,1:T(8,128)S(1)} %get-tuple-element.18), channel_id=1, source_target_pairs={{0,4},{4,8},{8,12},{12,16},{16,20},{20,24},{24,28},{1,5},{5,9},{9,... | collective-permute-start | bytes 393224 | tf_op jit(solution)/shard_map/ppermute | solution.py:26
  119.7 17.3 %copy-start.4 = (f32[128]{0:T(128)S(1)}, f32[128]{0:T(128)}, u32[]{:S(2)}) copy-start(f32[128]{0:T(128)} %param.15) | copy-start | bytes 1540
  119.7 17.3 %copy-start.6 = (f32[128]{0:T(128)S(1)}, f32[128]{0:T(128)}, u32[]{:S(2)}) copy-start(f32[128]{0:T(128)} %param.14) | copy-start | bytes 1540
  123.5 7.1 %all-to-all-start = ((f32[4,1,1024]{2,1,0:T(1,128)}), f32[4,1,1024]{2,1,0:T(1,128)S(1)}, u32[]{:S(2)}, u32[]{:S(2)}) async-start(f32[4,1,1024]{2,1,0:T(1,128)} %reshape.71), calls=%async_computation | async-start | bytes 32768 | tf_op jit(solution)/shard_map/all_to_all | solution.py:102
  130.5 138.8 %all-to-all-start.1 = ((f32[4,32,8,256]{3,1,2,0:T(8,128)}), f32[4,32,8,256]{3,1,2,0:T(8,128)S(1)}, u32[]{:S(2)}, u32[]{:S(2)}) async-start(f32[4,32,8,256]{3,1,2,0:T(8,128)} %pad_maximum_fusion.16), calls=%async_computation.1 | async-start | bytes 2097152 | tf_op jit(solution)/shard_map/all_to_all | solution.py:13
  134.1 124.0 %all-reduce.18.cloned.1.call-start = ((), (), s32[]{:S(2)}) async-start(), calls=%async_computation.3 | async-start | bytes 131072 | tf_op jit(solution)/shard_map/psum | solution.py:107
Sparse Core Ops, SparseCore 0:
  140.5 117.4 all-reduce.17
